TPU v7x, 32 devices: a whole 2x2x4 slice. The times are simulated.
32 devices in a mesh: rep: 8 (over z, y), tp: 4 (over x, core).
Axes of the slice: x: 2, y: 2, z: 4, core: 2. Of those that a mesh axis runs over, the one named last changes fastest.
Arguments:
- image_grads: bfloat16 [32, 48, 1280], P('rep', 'tp'), may hold values from -6 to 6
- dest_rank: int32 [32], P('rep'), may hold values from 0 to 7, as said below
- dest_slot: int32 [32], P('rep'), may hold values from 0 to 7, as said below
- saved_inputs: bfloat16 [64, 48, 1280], P('rep'), may hold values from -6 to 6
- up_weight: bfloat16 [1280, 5120], P(None, 'tp'), may hold values from -0.15625 to 0.15625
- down_weight: bfloat16 [5120, 1280], P('tp'), may hold values from -0.078125 to 0.078125
- norm_gain: float32 [1280], replicated, may hold values from 0.25 to 1.75
Outputs:
- input_grads: bfloat16 [64, 48, 1280], P('rep', 'tp')
- up_grads: float32 [1280, 5120], P('rep', 'tp')
- down_grads: float32 [5120, 1280], P('tp', 'rep')
- gain_grads: float32 [1280], replicated
Inputs may be any that keep to these rules, and one draw needn't show every extreme that they name: `dest_rank`: the images of one index of rep go to different owners; each owner receives at most 8 images, and some owner receives exactly 8 in every draw. `dest_slot`: the images that one owner receives have distinct slots 0, 1, ... up to their count less one; other slots hold no image.
All inputs are finite; a program needn't handle non-finite values.
Results may differ from a plain program's by a relative error of at most 0.015.
Values may be sent and summed in bfloat16 or wider, within the bound.
No kernel may reach another device: no remote copies, remote signals or barrier semaphores. Data moves between devices by JAX's collectives and lax.ppermute only.
A program may use at most 128 MiB of HBM per device.

v0:
```python
import jax
import jax.numpy as jnp
from jax import lax
from jax.sharding import PartitionSpec as P

epsilon = 1e-05
gelu_c = 0.7978845608028654
gelu_a = 0.044715


def gelu_value(preact):
    inner = jnp.tanh(gelu_c * (preact + gelu_a * preact**3))
    return 0.5 * preact * (1.0 + inner)


def gelu_slope(preact):
    inner = jnp.tanh(gelu_c * (preact + gelu_a * preact**3))
    return 0.5 * (1.0 + inner) + 0.5 * preact * (1.0 - inner * inner) * gelu_c * (
        1.0 + 3.0 * gelu_a * preact * preact
    )


def outbound(images, dest_rank, dest_slot, groups, capacity):
    rank_ids = jnp.arange(groups, dtype=jnp.int32)
    one_hot = dest_rank[None, :] == rank_ids[:, None]
    packed = jnp.einsum(
        "ek,kpd->epd", one_hot.astype(jnp.bfloat16), images, preferred_element_type=jnp.float32
    ).astype(jnp.bfloat16)
    present = jnp.any(one_hot, axis=1)
    slot_sent = jnp.sum(jnp.where(one_hot, dest_slot[None, :], 0), axis=1) + jnp.where(
        present, 0, capacity
    )
    return (packed, slot_sent)


def compact(inbound, slot_recv, capacity):
    slot_ids = jnp.arange(capacity, dtype=jnp.int32)
    picker = (slot_recv[None, :] == slot_ids[:, None]).astype(jnp.bfloat16)
    return jnp.einsum("ce,epd->cpd", picker, inbound, preferred_element_type=jnp.float32).astype(
        jnp.bfloat16
    )


def local(image_grads, dest_rank, dest_slot, saved_inputs, up_weight, down_weight, norm_gain):
    groups = lax.axis_size("rep")
    capacity = saved_inputs.shape[0]
    patches = saved_inputs.shape[1]
    width = saved_inputs.shape[2]
    slab = image_grads.shape[1]
    packed, slot_sent = outbound(image_grads, dest_rank, dest_slot, groups, capacity)
    inbound, slot_recv = (
        lax.all_to_all(packed, "rep", split_axis=0, concat_axis=0, tiled=True),
        lax.all_to_all(slot_sent, "rep", split_axis=0, concat_axis=0, tiled=True),
    )
    routed = lax.all_gather(compact(inbound, slot_recv, capacity), "tp", axis=1, tiled=True)
    rows = capacity * patches
    grads = routed.reshape(rows, width)
    values = saved_inputs.reshape(rows, width).astype(jnp.float32)
    mean_v = jnp.mean(values, axis=1, keepdims=True)
    var_v = jnp.mean((values - mean_v) ** 2, axis=1, keepdims=True)
    inv_std = 1.0 / jnp.sqrt(var_v + epsilon)
    centred = (values - mean_v) * inv_std
    normed = (centred * norm_gain[None, :]).astype(jnp.bfloat16)
    preact = jnp.dot(normed, up_weight, preferred_element_type=jnp.float32)
    hidden = gelu_value(preact).astype(jnp.bfloat16)
    grad_hidden = jnp.dot(grads, down_weight.T, preferred_element_type=jnp.float32)
    grad_pre = (grad_hidden * gelu_slope(preact)).astype(jnp.bfloat16)
    down_local = jnp.dot(hidden.T, grads, preferred_element_type=jnp.float32)
    up_local = jnp.dot(normed.T, grad_pre, preferred_element_type=jnp.float32)
    partial_normed = jnp.dot(grad_pre, up_weight.T, preferred_element_type=jnp.float32)
    up_grads, down_grads = (
        lax.psum_scatter(
            up_local.astype(jnp.bfloat16), "rep", scatter_dimension=0, tiled=True
        ).astype(jnp.float32),
        lax.psum_scatter(
            down_local.astype(jnp.bfloat16), "rep", scatter_dimension=1, tiled=True
        ).astype(jnp.float32),
    )
    start = lax.axis_index("tp") * slab
    grad_normed = lax.psum(partial_normed.astype(jnp.bfloat16), "tp").astype(jnp.float32)
    gain_grads = lax.psum(jnp.sum(grad_normed * centred, axis=0), "rep")
    scaled = grad_normed * norm_gain[None, :]
    first = jnp.mean(scaled, axis=1, keepdims=True)
    second = jnp.mean(scaled * centred, axis=1, keepdims=True)
    result = grads.astype(jnp.float32) + inv_std * (scaled - first - centred * second)
    result = result.reshape(capacity, patches, width)
    input_grads = lax.dynamic_slice_in_dim(result, start, slab, 1).astype(jnp.bfloat16)
    return (input_grads, up_grads, down_grads, gain_grads)


def solution(mesh):
    in_specs = (
        P("rep", "tp", None),
        P("rep"),
        P("rep"),
        P("rep", None, None),
        P(None, "tp"),
        P("tp", None),
        P(),
    )
    out_specs = (P("rep", "tp", None), P("rep", "tp"), P("tp", "rep"), P())
    return jax.shard_map(local, mesh=mesh, in_specs=in_specs, out_specs=out_specs, check_vma=False)
```

profile of v0, /device:TPU:0, one launch (start us, length us, event | category | flops | bytes accessed | tf_op | source)
XLA Modules:
  0.0 227.4 jit_solution(4812168266985921151)
XLA Ops:
  8.0 0.9 fusion.26
  8.9 0.9 select_reduce_fusion
  9.9 0.7 copy.19
  10.5 7.3 %all-to-all-start = ((s32[8,1,1]{2,1,0:T(1,128)}), s32[8,1,1]{2,1,0:T(1,128)S(1)}, u32[]{:S(2)}, u32[]{:S(2)}) async-start(s32[8,1,1]{2,1,0:T(1,128)} %copy.19), calls=%async_computation | async-start | bytes 8192 | tf_op jit(solution)/shard_map/all_to_all | solution.py:53
  17.8 1.4 convert_reduce_fusion
  19.3 1.6 multiply_reduce_fusion
  21.1 0.3 convolution_convert_fusion.4
  21.4 2.5 %multiply_convert_fusion.1 = bf16[384,1280]{1,0:T(8,128)(2,1)} fusion(bf16[8,48,1280]{2,1,0:T(8,128)(2,1)} %param.10, f32[1280]{0:T(1024)S(1)} %copy-done.5, f32[384]{0:T(512)S(1)} %div.18, f32[384]{0:T(512)S(1)} %sqrt.6), kind=kLoop, calls=%fused_computation.29 | loop fusion | flops 2457600 | bytes 1974272 | tf_op jit(solution)/shard_map/convert_element_type | solution.py:63
  23.9 0.8 copy.20
  24.7 6.0 %all-to-all-start.1 = ((bf16[8,12,1280]{2,1,0:T(8,128)(2,1)}), bf16[8,12,1280]{2,1,0:T(8,128)(2,1)}, u32[]{:S(2)}, u32[]{:S(2)}) async-start(bf16[8,12,1280]{2,1,0:T(8,128)(2,1)} %copy.20), calls=%async_computation.1 | async-start | bytes 655360 | tf_op jit(solution)/shard_map/all_to_all | solution.py:52
  30.7 4.0 %fusion.33 = f32[384,1280]{1,0:T(8,128)} fusion(bf16[384,1280]{1,0:T(8,128)(2,1)} %multiply_convert_fusion.1, bf16[1280,1280]{1,0:T(8,128)(2,1)S(1)} %copy-done), kind=kOutput, calls=%fused_computation.56 | convolution fusion | flops 1258291200 | bytes 6225920 | tf_op jit(solution)/shard_map/dot_general | solution.py:64
  34.7 0.2 reduce.2
  34.9 5.6 %all-to-all-done.1 = bf16[8,12,1280]{2,1,0:T(8,128)(2,1)} async-done(((bf16[8,12,1280]{2,1,0:T(8,128)(2,1)}), bf16[8,12,1280]{2,1,0:T(8,128)(2,1)}, u32[]{:S(2)}, u32[]{:S(2)}) %all-to-all-start.1) | async-done | bytes 245792 | tf_op jit(solution)/shard_map/all_to_all | solution.py:52
  40.5 1.3 convolution_convert_fusion.3
  41.9 9.7 %all_gather.3 = bf16[8,48,1280]{2,0,1:T(8,128)(2,1)S(1)} all-gather(bf16[8,12,1280]{2,0,1:T(8,128)(2,1)S(1)} %convolution_convert_fusion.3), channel_id=1, replica_groups=mesh['rep'=8,'tp'=4] {'tp'}, dimensions={1}, use_global_device_ids=true | all-gather | bytes 1228800 | tf_op jit(solution)/shard_map/all_gather | solution.py:55
  51.5 0.2 copy.22
  51.7 3.8 %fusion = bf16[384,1280]{1,0:T(8,128)(2,1)S(1)} fusion(bf16[384,1280]{1,0:T(8,128)(2,1)S(1)} %bitcast.33, bf16[1280,1280]{1,0:T(8,128)(2,1)S(1)} %copy-done.7, f32[384,1280]{1,0:T(8,128)} %fusion.33), kind=kOutput, calls=%fused_computation.5 | convolution fusion | flops 1267630080 | bytes 7208960 | tf_op jit(solution)/shard_map/dot_general | solution.py:66
  55.6 0.9 copy-done.8
  56.5 2.4 %convolution_convert_fusion.2 = bf16[384,1280]{1,0:T(8,128)(2,1)} fusion(bf16[384,1280]{1,0:T(8,128)(2,1)S(1)} %fusion, bf16[1280,1280]{1,0:T(8,128)(2,1)S(1)} %copy-done), kind=kOutput, calls=%fused_computation.6 | convolution fusion | flops 1258782720 | bytes 5242880 | tf_op jit(solution)/shard_map/dot_general | solution.py:70
  59.0 5.1 %convolution_convert_fusion.1 = bf16[1280,1280]{1,0:T(8,128)(2,1)} fusion(bf16[384,1280]{1,0:T(8,128)(2,1)} %multiply_convert_fusion.1, bf16[384,1280]{1,0:T(8,128)(2,1)} %copy-done.8), kind=kOutput, calls=%fused_computation.1 | convolution fusion | flops 1259929600 | bytes 5242880 | tf_op jit(solution)/shard_map/dot_general | solution.py:69
  64.1 0.2 reduce-scatter.5.cloned.1.call-start
  64.4 5.5 %convolution_convert_fusion = bf16[1280,1280]{0,1:T(8,128)(2,1)} fusion(bf16[384,1280]{1,0:T(8,128)(2,1)} %bitcast.34, f32[384,1280]{1,0:T(8,128)} %fusion.33), kind=kOutput, calls=%fused_computation | convolution fusion | flops 1264353280 | bytes 6225920 | tf_op jit(solution)/shard_map/dot_general | solution.py:68
  69.9 23.6 %all-reduce.2.cloned.1.call-done = bf16[384,1280]{1,0:T(8,128)(2,1)} async-done(((bf16[384,1280]{1,0:T(8,128)(2,1)}), bf16[384,1280]{1,0:T(8,128)(2,1)}) %all-reduce.2.cloned.1.call-update) | async-done | bytes 983056 | tf_op jit(solution)/shard_map/psum | solution.py:80
  93.5 2.6 %fusion.8 = (f32[1280]{0:T(1024)S(1)}, f32[384]{0:T(512)S(1)}, f32[384]{0:T(512)S(1)}) fusion(bf16[384,1280]{1,0:T(8,128)(2,1)} %all-reduce.2.cloned.1.call-done, bf16[8,48,1280]{2,1,0:T(8,128)(2,1)} %param.10, f32[384]{0:T(512)S(1)} %div.18, f32[384]{0:T(512)S(1)} %sqrt.6, f32[1280]{0:T(1024)S(1)} %copy-done.5), kind=kLoop, calls=%fused_computation.18 | loop fusion | flops 4913152 | bytes 1982464 | tf_op jit(solution)/shard_map/reduce_sum | solution.py:81
  96.1 2.1 fusion.6
  98.2 0.1 constant_dynamic-slice_fusion
  98.3 0.8 copy.28
  99.0 22.1 %psum.15 = f32[1280]{0:T(1024)} all-reduce(f32[1280]{0:T(1024)S(1)} %get-tuple-element.4), channel_id=1, replica_groups=mesh['rep'=8,'tp'=4] {'rep'}, use_global_device_ids=true, to_apply=%region_10.11 | all-reduce | flops 1280 | bytes 10240 | tf_op jit(solution)/shard_map/psum | solution.py:81
  121.2 18.0 %reduce-scatter.3.cloned.1.call-done = bf16[160,1280]{1,0:T(8,128)(2,1)} async-done(((bf16[1280,1280]{1,0:T(8,128)(2,1)}), bf16[160,1280]{1,0:T(8,128)(2,1)}) %reduce-scatter.3.cloned.1.call-update) | async-done | bytes 409616 | tf_op jit(solution)/shard_map/reduce_scatter | solution.py:72
  139.2 1.9 convert_element_type.63
  141.1 76.9 %reduce-scatter.5.cloned.1.call-done = bf16[1280,160]{0,1:T(8,128)(2,1)} async-done(((bf16[1280,1280]{0,1:T(8,128)(2,1)}), bf16[1280,160]{0,1:T(8,128)(2,1)}) %reduce-scatter.5.cloned.1.call-update) | async-done | bytes 409616 | tf_op jit(solution)/shard_map/reduce_scatter | solution.py:75
  218.0 1.9 convert_element_type.66
  (29 shorter events, 0.4 us)
Async XLA Ops:
  8.0 22.7 %copy-start = (bf16[1280,1280]{1,0:T(8,128)(2,1)S(1)}, bf16[1280,1280]{1,0:T(8,128)(2,1)}, u32[]{:S(2)}) copy-start(bf16[1280,1280]{1,0:T(8,128)(2,1)} %param.11) | copy-start | bytes 9830404
  8.0 13.0 %copy-start.6 = (s32[4]{0:T(128)S(1)}, s32[4]{0:T(128)}, u32[]{:S(2)}) copy-start(s32[4]{0:T(128)} %param.8) | copy-start | bytes 52
  8.0 13.0 %copy-start.4 = (bf16[4,12,1280]{2,0,1:T(4,128)(2,1)S(1)}, bf16[4,12,1280]{2,0,1:T(4,128)(2,1)}, u32[]{:S(2)}) copy-start(bf16[4,12,1280]{2,0,1:T(4,128)(2,1)} %param.7) | copy-start | bytes 368644
  8.0 13.4 %copy-start.5 = (f32[1280]{0:T(1024)S(1)}, f32[1280]{0:T(1024)}, u32[]{:S(2)}) copy-start(f32[1280]{0:T(1024)} %param.13) | copy-start | bytes 15364
  10.5 14.2 %all-to-all-start = ((s32[8,1,1]{2,1,0:T(1,128)}), s32[8,1,1]{2,1,0:T(1,128)S(1)}, u32[]{:S(2)}, u32[]{:S(2)}) async-start(s32[8,1,1]{2,1,0:T(1,128)} %copy.19), calls=%async_computation | async-start | bytes 8192 | tf_op jit(solution)/shard_map/all_to_all | solution.py:53
  24.7 15.8 %all-to-all-start.1 = ((bf16[8,12,1280]{2,1,0:T(8,128)(2,1)}), bf16[8,12,1280]{2,1,0:T(8,128)(2,1)}, u32[]{:S(2)}, u32[]{:S(2)}) async-start(bf16[8,12,1280]{2,1,0:T(8,128)(2,1)} %copy.20), calls=%async_computation.1 | async-start | bytes 655360 | tf_op jit(solution)/shard_map/all_to_all | solution.py:52
  30.7 62.8 %all-reduce.2.cloned.1.call-start = ((), (), s32[]{:S(2)}) async-start(), calls=%async_computation.4 | async-start | bytes 1966080 | tf_op jit(solution)/shard_map/psum | solution.py:80
  40.5 11.2 %copy-start.7 = (bf16[1280,1280]{1,0:T(8,128)(2,1)S(1)}, bf16[1280,1280]{1,0:T(8,128)(2,1)}, u32[]{:S(2)}) copy-start(bf16[1280,1280]{1,0:T(8,128)(2,1)} %param.12) | copy-start | bytes 9830404
  51.7 3.9 %copy-start.2 = (bf16[8,48,1280]{2,1,0:T(8,128)(2,1)}, bf16[8,48,1280]{2,1,0:T(8,128)(2,1)S(1)}, u32[]{:S(2)}) copy-start(bf16[8,48,1280]{2,1,0:T(8,128)(2,1)S(1)} %copy.22) | copy-start | bytes 2949124
  55.6 1.0 copy-start.8
  59.0 80.2 %reduce-scatter.3.cloned.1.call-start = ((), (), s32[]{:S(2)}) async-start(), calls=%async_computation.5 | async-start | bytes 3686400 | tf_op jit(solution)/shard_map/reduce_scatter | solution.py:72
  64.1 153.9 %reduce-scatter.5.cloned.1.call-start = ((), (), s32[]{:S(2)}) async-start(), calls=%async_computation.6 | async-start | bytes 3686400 | tf_op jit(solution)/shard_map/reduce_scatter | solution.py:75
  93.5 2.6 %copy-start.1 = (bf16[8,48,1280]{2,1,0:T(8,128)(2,1)S(1)}, bf16[8,48,1280]{2,1,0:T(8,128)(2,1)}, u32[]{:S(2)}) copy-start(bf16[8,48,1280]{2,1,0:T(8,128)(2,1)} %param.10) | copy-start | bytes 2949124
  93.5 2.6 %copy-start.3 = (bf16[8,48,1280]{2,1,0:T(8,128)(2,1)S(1)}, bf16[8,48,1280]{2,1,0:T(8,128)(2,1)}, u32[]{:S(2)}) copy-start(bf16[8,48,1280]{2,1,0:T(8,128)(2,1)} %copy-done.2) | copy-start | bytes 2949124
Sparse Core Ops, SparseCore 0:
  59.1 34.3 all-reduce.1
Sparse Core Ops, SparseCore 1:
  64.2 74.9 reduce-scatter.2
  142.6 75.3 reduce-scatter.4
where the time goes:
time: 228 us; the launch traced here: 227 us
  waiting for transfers between devices  124 us (54%)
  blocking collectives  31.8 us (14%)
  matrix products  22.5 us (10%)
  other arithmetic  16.1 us (7%)
  between operations  15.7 us (7%)
  starting transfers between devices  13.6 us (6%)
  local copies, waits for them, and re-layouts  3.62 us (2%)
    reduce_scatter x1, waiting for transfers between devices, local(): lax.psum_scatter(down_local.astype(jnp.bfloat16), 'rep', scatter_dimensio...  76.9 us
    psum x1, waiting for transfers between devices, local(): lax.psum(partial_normed.astype(jnp.bfloat16), 'tp').astype(jnp.float32)  23.6 us
    psum x1, blocking collectives, local(): gain_grads = lax.psum(jnp.sum(grad_normed * centred, axis=0), 'rep')  22.1 us
    reduce_scatter x1, waiting for transfers between devices, local(): lax.psum_scatter(up_local.astype(jnp.bfloat16), 'rep', scatter_dimension=...  18 us
    all_gather x1, blocking collectives, local(): lax.all_gather(compact(inbound, slot_recv, capacity), 'tp', axis=1, tiled...  9.67 us
    all_to_all x1, starting transfers between devices, local(): lax.all_to_all(slot_sent, 'rep', split_axis=0, concat_axis=0, tiled=True)  7.31 us
    all_to_all x1, starting transfers between devices, local(): lax.all_to_all(packed, 'rep', split_axis=0, concat_axis=0, tiled=True)  6 us
    all_to_all x1, waiting for transfers between devices, local(): lax.all_to_all(packed, 'rep', split_axis=0, concat_axis=0, tiled=True)  5.58 us
  transfers between devices with their start and end apart: 5, of which 4 were waited for; matrix products, arithmetic and copies ran while one was open for 13% of the time, Pallas kernels for 0%

commit v1 on v0

--- a/solution.py
+++ b/solution.py
@@ -52,7 +52,20 @@
         lax.all_to_all(packed, "rep", split_axis=0, concat_axis=0, tiled=True),
         lax.all_to_all(slot_sent, "rep", split_axis=0, concat_axis=0, tiled=True),
     )
-    routed = lax.all_gather(compact(inbound, slot_recv, capacity), "tp", axis=1, tiled=True)
+    x = compact(inbound, slot_recv, capacity)
+    ways, here, step = (lax.axis_size("tp"), lax.axis_index("tp"), x.shape[1])
+    shape = [n * ways if d == 1 else n for d, n in enumerate(x.shape)]
+    full = lax.dynamic_update_slice_in_dim(jnp.zeros(shape, x.dtype), x, here * step, axis=1)
+    going_up = going_down = x
+    for far in range(1, ways // 2 + 1):
+        going_up = lax.ppermute(going_up, "tp", [(d, (d + 1) % ways) for d in range(ways)])
+        full = lax.dynamic_update_slice_in_dim(full, going_up, (here - far) % ways * step, axis=1)
+        if 2 * far < ways:
+            going_down = lax.ppermute(going_down, "tp", [(d, (d - 1) % ways) for d in range(ways)])
+            full = lax.dynamic_update_slice_in_dim(
+                full, going_down, (here + far) % ways * step, axis=1
+            )
+    routed = full
     rows = capacity * patches
     grads = routed.reshape(rows, width)
     values = saved_inputs.reshape(rows, width).astype(jnp.float32)

time: 228 us -> 247 us (1.083)
  local copies, waits for them, and re-layouts: 3.62 us -> 24.1 us
  blocking collectives: 31.8 us -> 22.2 us
  waiting for transfers between devices: 124 us -> 130 us
    dynamic_update_slice x0 -> x4, local copies, waits for them, and re-layouts: none -> 13.8 us  [the longest x2 6.57 us: local(): lax.dynamic_update_slice_in_dim(full, going_up, (here - far) % ways * ste...]
    all_gather x1 -> x0, blocking collectives: 9.67 us -> none  [local(): lax.all_gather(compact(inbound, slot_recv, capacity), 'tp', axis=1, tiled...]
    ppermute x0 -> x3, local copies, waits for them, and re-layouts: none -> 5.14 us  [the longest x2 3.43 us: local(): lax.ppermute(going_up, 'tp', [(d, (d + 1) % ways) for d in range(ways)])]
    all_to_all x1, waiting for transfers between devices: 0.01 us -> 2.98 us  [local(): lax.all_to_all(slot_sent, 'rep', split_axis=0, concat_axis=0, tiled=True)]
  transfers between devices with their start and end apart: 5 -> 8, of which waited for: 4 -> 6; matrix products, arithmetic and copies ran while one was open for 13% -> 18% of each run, Pallas kernels for 0% -> 0%
where the time goes in v1:
time: 247 us; the launch traced here: 246 us
  waiting for transfers between devices  130 us (53%)
  matrix products  24.2 us (10%)
  local copies, waits for them, and re-layouts  24.1 us (10%)
  blocking collectives  22.2 us (9%)
  other arithmetic  16.1 us (7%)
  between operations  15.6 us (6%)
  starting transfers between devices  13.5 us (5%)
    reduce_scatter x1, waiting for transfers between devices, local(): lax.psum_scatter(down_local.astype(jnp.bfloat16), 'rep', scatter_dimensio...  76.5 us
    psum x1, waiting for transfers between devices, local(): lax.psum(partial_normed.astype(jnp.bfloat16), 'tp').astype(jnp.float32)  24.7 us
    psum x1, blocking collectives, local(): gain_grads = lax.psum(jnp.sum(grad_normed * centred, axis=0), 'rep')  22.2 us
    reduce_scatter x1, waiting for transfers between devices, local(): lax.psum_scatter(up_local.astype(jnp.bfloat16), 'rep', scatter_dimension=...  17.7 us
    all_to_all x1, starting transfers between devices, local(): lax.all_to_all(slot_sent, 'rep', split_axis=0, concat_axis=0, tiled=True)  7.31 us
    all_to_all x1, waiting for transfers between devices, local(): lax.all_to_all(packed, 'rep', split_axis=0, concat_axis=0, tiled=True)  7.08 us
    dynamic_update_slice x2, local copies, waits for them, and re-layouts, local(): lax.dynamic_update_slice_in_dim(full, going_up, (here - far) % ways * ste...  6.57 us
    dot_general x1, matrix products, local(): down_local = jnp.dot(hidden.T, grads, preferred_element_type=jnp.float32)  5.53 us
  transfers between devices with their start and end apart: 8, of which 6 were waited for; matrix products, arithmetic and copies ran while one was open for 18% of the time, Pallas kernels for 0%

profile of v1, /device:TPU:0, one launch (start us, length us, event | category | flops | bytes accessed | tf_op | source)
XLA Modules:
  0.0 246.2 jit_solution(9314961075651744254)
XLA Ops:
  10.4 7.3 %all-to-all-start = ((s32[8,1,1]{2,1,0:T(1,128)}), s32[8,1,1]{2,1,0:T(1,128)S(1)}, u32[]{:S(2)}, u32[]{:S(2)}) async-start(s32[8,1,1]{2,1,0:T(1,128)} %copy.23), calls=%async_computation | async-start | bytes 8192 | tf_op jit(solution)/shard_map/all_to_all | solution.py:53
  17.8 1.2 convolution_convert_fusion.4
  19.0 1.4 convert_reduce_fusion
  21.2 3.0 %all-to-all-done = s32[8,1,1]{2,1,0:T(1,128)S(1)} async-done(((s32[8,1,1]{2,1,0:T(1,128)}), s32[8,1,1]{2,1,0:T(1,128)S(1)}, u32[]{:S(2)}, u32[]{:S(2)}) %all-to-all-start) | async-done | bytes 64 | tf_op jit(solution)/shard_map/all_to_all | solution.py:53
  24.2 4.1 %all-to-all-start.1 = ((bf16[8,12,1280]{2,1,0:T(8,128)(2,1)}), bf16[8,12,1280]{2,1,0:T(8,128)(2,1)}, u32[]{:S(2)}, u32[]{:S(2)}) async-start(bf16[8,12,1280]{2,1,0:T(8,128)(2,1)} %copy.24), calls=%async_computation.1 | async-start | bytes 655360 | tf_op jit(solution)/shard_map/all_to_all | solution.py:52
  28.4 1.6 multiply_reduce_fusion
  30.3 7.1 %all-to-all-done.1 = bf16[8,12,1280]{2,1,0:T(8,128)(2,1)} async-done(((bf16[8,12,1280]{2,1,0:T(8,128)(2,1)}), bf16[8,12,1280]{2,1,0:T(8,128)(2,1)}, u32[]{:S(2)}, u32[]{:S(2)}) %all-to-all-start.1) | async-done | bytes 245792 | tf_op jit(solution)/shard_map/all_to_all | solution.py:52
  37.4 1.2 convolution_convert_fusion.3
  38.7 2.5 %multiply_convert_fusion.1 = bf16[384,1280]{1,0:T(8,128)(2,1)} fusion(bf16[8,48,1280]{2,1,0:T(8,128)(2,1)} %param.10, f32[1280]{0:T(1024)S(1)} %copy-done.3, f32[384]{0:T(512)S(1)} %div.18, f32[384]{0:T(512)S(1)} %sqrt.6), kind=kLoop, calls=%fused_computation.29 | loop fusion | flops 2457600 | bytes 1974272 | tf_op jit(solution)/shard_map/convert_element_type | solution.py:76
  41.2 1.7 collective-permute-start.1
  42.9 1.5 collective-permute-done
  44.4 4.0 %fusion.33 = f32[384,1280]{1,0:T(8,128)} fusion(bf16[384,1280]{1,0:T(8,128)(2,1)} %multiply_convert_fusion.1, bf16[1280,1280]{1,0:T(8,128)(2,1)S(1)} %copy-done), kind=kOutput, calls=%fused_computation.56 | convolution fusion | flops 1258291200 | bytes 6225920 | tf_op jit(solution)/shard_map/dot_general | solution.py:77
  49.1 1.0 broadcast_in_dim.22
  50.1 3.6 %dynamic_update_slice.12 = bf16[8,48,1280]{2,1,0:T(8,128)(2,1)} dynamic-update-slice(bf16[8,48,1280]{2,1,0:T(8,128)(2,1)} %broadcast_in_dim.22, bf16[8,12,1280]{2,1,0:T(8,128)(2,1)} %copy.26, s32[]{:T(128)} %constant.45.clone.1, s32[]{:T(128)S(6)} %select_n.46, s32[]{:T(128)} %constant.45.clone.1) | dynamic-update-slice | bytes 491524 | tf_op jit(solution)/shard_map/dynamic_update_slice | solution.py:58
  53.7 1.7 copy.27
  55.4 3.0 %dynamic_update_slice.13 = bf16[8,48,1280]{2,1,0:T(8,128)(2,1)} dynamic-update-slice(bf16[8,48,1280]{2,1,0:T(8,128)(2,1)} %dynamic_update_slice.12, bf16[8,12,1280]{2,1,0:T(8,128)(2,1)} %copy.27, s32[]{:T(128)} %constant.45.clone.1, s32[]{:T(128)S(6)} %select_n.48, s32[]{:T(128)} %constant.45.clone.1) | dynamic-update-slice | bytes 491524 | tf_op jit(solution)/shard_map/dynamic_update_slice | solution.py:62
  58.5 1.7 copy.28
  60.2 3.6 %dynamic_update_slice.14 = bf16[8,48,1280]{2,1,0:T(8,128)(2,1)} dynamic-update-slice(bf16[8,48,1280]{2,1,0:T(8,128)(2,1)} %dynamic_update_slice.13, bf16[8,12,1280]{2,1,0:T(8,128)(2,1)} %copy.28, s32[]{:T(128)} %constant.45.clone.1, s32[]{:T(128)S(6)} %select_n.50, s32[]{:T(128)} %constant.45.clone.1) | dynamic-update-slice | bytes 491524 | tf_op jit(solution)/shard_map/dynamic_update_slice | solution.py:65
  63.8 1.7 copy.29
  65.5 3.5 %dynamic_update_slice.15 = bf16[8,48,1280]{2,1,0:T(8,128)(2,1)} dynamic-update-slice(bf16[8,48,1280]{2,1,0:T(8,128)(2,1)} %dynamic_update_slice.14, bf16[8,12,1280]{2,1,0:T(8,128)(2,1)} %copy.29, s32[]{:T(128)} %constant.45.clone.1, s32[]{:T(128)S(6)} %select_n.52, s32[]{:T(128)} %constant.45.clone.1) | dynamic-update-slice | bytes 491524 | tf_op jit(solution)/shard_map/dynamic_update_slice | solution.py:62
  69.1 4.8 %fusion = bf16[384,1280]{1,0:T(8,128)(2,1)S(1)} fusion(bf16[384,1280]{1,0:T(8,128)(2,1)} %bitcast.33, bf16[1280,1280]{1,0:T(8,128)(2,1)} %param.12, f32[384,1280]{1,0:T(8,128)} %fusion.33), kind=kOutput, calls=%fused_computation.5 | convolution fusion | flops 1267630080 | bytes 7208960 | tf_op jit(solution)/shard_map/dot_general | solution.py:79
  74.8 2.4 convolution_convert_fusion.2
  77.3 5.1 %convolution_convert_fusion.1 = bf16[1280,1280]{1,0:T(8,128)(2,1)} fusion(bf16[384,1280]{1,0:T(8,128)(2,1)} %multiply_convert_fusion.1, bf16[384,1280]{1,0:T(8,128)(2,1)} %copy-done.4), kind=kOutput, calls=%fused_computation.1 | convolution fusion | flops 1259929600 | bytes 5242880 | tf_op jit(solution)/shard_map/dot_general | solution.py:82
  82.6 5.5 %convolution_convert_fusion = bf16[1280,1280]{0,1:T(8,128)(2,1)} fusion(bf16[384,1280]{1,0:T(8,128)(2,1)} %bitcast.34, f32[384,1280]{1,0:T(8,128)} %fusion.33), kind=kOutput, calls=%fused_computation | convolution fusion | flops 1264353280 | bytes 6225920 | tf_op jit(solution)/shard_map/dot_general | solution.py:81
  88.2 24.7 %all-reduce.2.cloned.1.call-done = bf16[384,1280]{1,0:T(8,128)(2,1)} async-done(((bf16[384,1280]{1,0:T(8,128)(2,1)}), bf16[384,1280]{1,0:T(8,128)(2,1)}) %all-reduce.2.cloned.1.call-update) | async-done | bytes 983056 | tf_op jit(solution)/shard_map/psum | solution.py:93
  112.9 2.6 %fusion.8 = (f32[1280]{0:T(1024)S(1)}, f32[384]{0:T(512)S(1)}, f32[384]{0:T(512)S(1)}) fusion(bf16[384,1280]{1,0:T(8,128)(2,1)} %all-reduce.2.cloned.1.call-done, bf16[8,48,1280]{2,1,0:T(8,128)(2,1)} %param.10, f32[384]{0:T(512)S(1)} %div.18, f32[384]{0:T(512)S(1)} %sqrt.6, f32[1280]{0:T(1024)S(1)} %copy-done.3), kind=kLoop, calls=%fused_computation.18 | loop fusion | flops 4913152 | bytes 1982464 | tf_op jit(solution)/shard_map/reduce_sum | solution.py:94
  115.5 2.1 fusion.6
  118.4 22.2 %psum.15 = f32[1280]{0:T(1024)} all-reduce(f32[1280]{0:T(1024)S(1)} %get-tuple-element.4), channel_id=1, replica_groups=mesh['rep'=8,'tp'=4] {'rep'}, use_global_device_ids=true, to_apply=%region_10.11 | all-reduce | flops 1280 | bytes 10240 | tf_op jit(solution)/shard_map/psum | solution.py:94
  140.7 17.7 %reduce-scatter.3.cloned.1.call-done = bf16[160,1280]{1,0:T(8,128)(2,1)} async-done(((bf16[1280,1280]{1,0:T(8,128)(2,1)}), bf16[160,1280]{1,0:T(8,128)(2,1)}) %reduce-scatter.3.cloned.1.call-update) | async-done | bytes 409616 | tf_op jit(solution)/shard_map/reduce_scatter | solution.py:85
  158.4 1.9 convert_element_type.63
  160.3 76.5 %reduce-scatter.5.cloned.1.call-done = bf16[1280,160]{0,1:T(8,128)(2,1)} async-done(((bf16[1280,1280]{0,1:T(8,128)(2,1)}), bf16[1280,160]{0,1:T(8,128)(2,1)}) %reduce-scatter.5.cloned.1.call-update) | async-done | bytes 409616 | tf_op jit(solution)/shard_map/reduce_scatter | solution.py:88
  236.8 1.9 convert_element_type.66
  (34 shorter events, 6.7 us)
Async XLA Ops:
  8.0 36.4 %copy-start = (bf16[1280,1280]{1,0:T(8,128)(2,1)S(1)}, bf16[1280,1280]{1,0:T(8,128)(2,1)}, u32[]{:S(2)}) copy-start(bf16[1280,1280]{1,0:T(8,128)(2,1)} %param.11) | copy-start | bytes 9830404
  10.4 13.7 %all-to-all-start = ((s32[8,1,1]{2,1,0:T(1,128)}), s32[8,1,1]{2,1,0:T(1,128)S(1)}, u32[]{:S(2)}, u32[]{:S(2)}) async-start(s32[8,1,1]{2,1,0:T(1,128)} %copy.23), calls=%async_computation | async-start | bytes 8192 | tf_op jit(solution)/shard_map/all_to_all | solution.py:53
  17.8 20.9 %copy-start.3 = (f32[1280]{0:T(1024)S(1)}, f32[1280]{0:T(1024)}, u32[]{:S(2)}) copy-start(f32[1280]{0:T(1024)} %param.13) | copy-start | bytes 15364
  24.2 13.2 %all-to-all-start.1 = ((bf16[8,12,1280]{2,1,0:T(8,128)(2,1)}), bf16[8,12,1280]{2,1,0:T(8,128)(2,1)}, u32[]{:S(2)}, u32[]{:S(2)}) async-start(bf16[8,12,1280]{2,1,0:T(8,128)(2,1)} %copy.24), calls=%async_computation.1 | async-start | bytes 655360 | tf_op jit(solution)/shard_map/all_to_all | solution.py:52
  28.3 84.6 %all-reduce.2.cloned.1.call-start = ((), (), s32[]{:S(2)}) async-start(), calls=%async_computation.4 | async-start | bytes 1966080 | tf_op jit(solution)/shard_map/psum | solution.py:93
  38.6 5.8 %collective-permute-start = (bf16[8,12,1280]{2,0,1:T(8,128)(2,1)S(1)}, bf16[8,12,1280]{2,0,1:T(8,128)(2,1)}, u32[]{:S(2)}, u32[]{:S(2)}) collective-permute-start(bf16[8,12,1280]{2,0,1:T(8,128)(2,1)S(1)} %convolution_convert_fusion.3), channel_id=1, source_target_pairs={{0,1},{1,2},{2,3},{3,0},{4,5},{5,6},{6,7},{7,4},{8,9},{9,10},{10,1... | collective-permute-start | bytes 737288 | tf_op jit(solution)/shard_map/ppermute | solution.py:61
  41.2 17.3 %collective-permute-start.1 = (bf16[8,12,1280]{2,0,1:T(8,128)(2,1)S(1)}, bf16[8,12,1280]{2,0,1:T(8,128)(2,1)}, u32[]{:S(2)}, u32[]{:S(2)}) collective-permute-start(bf16[8,12,1280]{2,0,1:T(8,128)(2,1)S(1)} %convolution_convert_fusion.3), channel_id=1, source_target_pairs={{0,3},{1,0},{2,1},{3,2},{4,7},{5,4},{6,5},{7,6},{8,11},{9,8},{10,9... | collective-permute-start | bytes 737288 | tf_op jit(solution)/shard_map/ppermute | solution.py:64
  44.4 19.4 %collective-permute-start.2 = (bf16[8,12,1280]{2,0,1:T(8,128)(2,1)}, bf16[8,12,1280]{2,0,1:T(8,128)(2,1)}, u32[]{:S(2)}, u32[]{:S(2)}) collective-permute-start(bf16[8,12,1280]{2,0,1:T(8,128)(2,1)} %collective-permute-done), channel_id=1, source_target_pairs={{0,1},{1,2},{2,3},{3,0},{4,5},{5,6},{6,7},{7,4},{8,9},{9,10},{10,1... | collective-permute-start | bytes 737288 | tf_op jit(solution)/shard_map/ppermute | solution.py:61
  73.8 1.0 copy-start.4
  77.2 81.1 %reduce-scatter.3.cloned.1.call-start = ((), (), s32[]{:S(2)}) async-start(), calls=%async_computation.5 | async-start | bytes 3686400 | tf_op jit(solution)/shard_map/reduce_scatter | solution.py:85
  82.4 154.4 %reduce-scatter.5.cloned.1.call-start = ((), (), s32[]{:S(2)}) async-start(), calls=%async_computation.6 | async-start | bytes 3686400 | tf_op jit(solution)/shard_map/reduce_scatter | solution.py:88
  112.9 2.6 %copy-start.1 = (bf16[8,48,1280]{2,1,0:T(8,128)(2,1)S(1)}, bf16[8,48,1280]{2,1,0:T(8,128)(2,1)}, u32[]{:S(2)}) copy-start(bf16[8,48,1280]{2,1,0:T(8,128)(2,1)} %param.10) | copy-start | bytes 2949124
  112.9 2.6 %copy-start.2 = (bf16[384,1280]{1,0:T(8,128)(2,1)S(1)}, bf16[384,1280]{1,0:T(8,128)(2,1)}, u32[]{:S(2)}) copy-start(bf16[384,1280]{1,0:T(8,128)(2,1)} %all-reduce.2.cloned.1.call-done) | copy-start | bytes 2949124
Sparse Core Ops, SparseCore 0:
  77.4 35.4 all-reduce.1
Sparse Core Ops, SparseCore 1:
  82.5 75.8 reduce-scatter.2
  161.8 74.9 reduce-scatter.4
